TPU v7x, 32 devices: a whole 2x2x4 slice. The times are simulated.
32 devices in a mesh: days: 4 (over y, x), assets: 8 (over z, core).
Axes of the slice: x: 2, y: 2, z: 4, core: 2. Of those that a mesh axis runs over, the one named last changes fastest.
Arguments:
- factors: bfloat16 [768, 256], P('days'), may hold values from -6 to 6
- returns: bfloat16 [768, 16384], P('days', 'assets'), may hold values from -6 to 6
Outputs:
- loadings: float32 [256, 16384], P(None, 'assets')
- covariance: float32 [16384, 16384], P('assets', 'days')
All inputs are finite; a program needn't handle non-finite values.
Results may differ from a plain program's by a relative error of at most 0.0036.
Values may be sent and summed in bfloat16 or wider, within the bound.
No kernel may reach another device: no remote copies, remote signals or barrier semaphores. Data moves between devices by JAX's collectives and lax.ppermute only.
A program may use at most 128 MiB of HBM per device.

v0:
```python
import jax
import jax.numpy as jnp
from jax import lax
from jax.sharding import PartitionSpec as P


def per_device(factors, returns):
    gram = lax.dot_general(
        factors, factors, (((0,), (0,)), ((), ())), preferred_element_type=jnp.float32
    )
    cross = lax.dot_general(
        factors, returns, (((0,), (0,)), ((), ())), preferred_element_type=jnp.float32
    )
    gram, cross = lax.psum((gram, cross), "days")
    lower = jnp.linalg.cholesky(gram)
    middle = lax.linalg.triangular_solve(lower, cross, left_side=True, lower=True)
    loadings = lax.linalg.triangular_solve(
        lower, middle, left_side=True, lower=True, transpose_a=True
    )
    fitted = jnp.dot(factors, loadings.astype(jnp.bfloat16), preferred_element_type=jnp.float32)
    residual = (returns.astype(jnp.float32) - fitted).astype(jnp.bfloat16)
    mine = lax.all_gather(residual, "days", axis=0, tiled=True)
    day_block = lax.all_gather(residual, "assets", axis=1, tiled=True)
    columns = lax.all_to_all(day_block, "days", split_axis=1, concat_axis=0, tiled=True)
    covariance = lax.dot_general(
        mine, columns, (((0,), (0,)), ((), ())), preferred_element_type=jnp.float32
    )
    covariance = covariance / mine.shape[0]
    return (loadings, covariance)


def solution(mesh):
    in_specs = (P("days", None), P("days", "assets"))
    out_specs = (P(None, "assets"), P("assets", "days"))
    return jax.shard_map(
        per_device, mesh=mesh, in_specs=in_specs, out_specs=out_specs, check_vma=False
    )
```

profile of v0, /device:TPU:0, one launch (start us, length us, event | category | flops | bytes accessed | tf_op | source)
XLA Modules:
  0.0 357.5 jit_solution(16672601659228201361)
XLA Ops:
  7.2 0.8 copy-done
  8.1 0.9 fusion.15
  9.0 2.9 fusion.16
  12.0 76.7 %all-reduce.4.cloned.1.call-done = (f32[256,2048]{1,0:T(8,128)}, f32[256,256]{0,1:T(8,128)}) async-done(((f32[256,2048]{1,0:T(8,128)}, f32[256,256]{0,1:T(8,128)}), (f32[256,2048]{1,0:T(8,128)}, f32[256,256]{0,1:T(8,128)})) %all-reduce.4.cloned.1.call-update) | async-done | bytes 2359312 | tf_op jit(solution)/shard_map/psum | solution.py:14
  88.7 1.2 copy.7
  89.9 1.0 fusion.5
  90.9 11.7 %cholesky.50 = f32[128,128]{1,0:T(8,128)S(1)} custom-call(f32[128,128]{1,0:T(8,128)S(1)} %cholesky.118), custom_call_target="Cholesky" | custom-call | tf_op jit(solution)/shard_map/jit(cholesky)/cholesky | solution.py:15
  102.7 9.8 %custom-call.16 = f32[1,128,128]{1,2,0:T(8,128)S(1)} custom-call(f32[1,128,128]{2,1,0:T(8,128)S(1)} %get-tuple-element.25), custom_call_target="InvertDiagBlocksLowerTriangular" | custom-call | tf_op jit(solution)/shard_map/jit(cholesky)/cholesky | solution.py:15
  112.7 0.3 convolution_subtract_fusion.2
  113.0 11.7 %cholesky.105 = f32[128,128]{1,0:T(8,128)S(1)} custom-call(f32[128,128]{1,0:T(8,128)S(1)} %convolution_subtract_fusion.2), custom_call_target="Cholesky" | custom-call | tf_op jit(solution)/shard_map/jit(cholesky)/cholesky | solution.py:15
  124.7 0.6 compare_reduce_fusion
  126.8 4.1 %while.1 = (s32[]{:T(128)}, f32[256,256]{1,0:T(8,128)S(1)}, s32[2,2]{1,0:T(2,128)S(1)}, f32[2,128,128]{2,1,0:T(8,128)S(1)}, s32[]{:T(128)}) while((s32[]{:T(128)}, f32[256,256]{1,0:T(8,128)S(1)}, s32[2,2]{1,0:T(2,128)S(1)}, f32[2,128,128]{2,1,0:T(8,128)S(1)}, s32[]{:T(128)}) %tuple.27), condition=%wide.while_cond, body=%wide.while_body.sunk | while | flops 2 | bytes 131189 | solution.py:17
  126.9 0.6 fusion.32
  127.5 1.4 bitcast_dynamic-update-slice_fusion.2
  129.0 0.6 fusion.32
  129.5 1.4 bitcast_dynamic-update-slice_fusion.2
  130.9 19.7 %custom-call.17 = f32[2,128,128]{1,2,0:T(8,128)S(1)} custom-call(f32[2,128,128]{2,1,0:T(8,128)S(1)} %get-tuple-element.9), custom_call_target="InvertDiagBlocksLowerTriangular" | custom-call | tf_op jit(solution)/shard_map/triangular_solve | solution.py:17
  150.6 1.1 fusion.2
  151.7 1.0 convolution_subtract_fusion.1
  152.7 1.1 fusion.11
  153.8 1.0 fusion.10
  154.8 1.0 convolution_subtract_fusion
  155.8 1.0 fusion.9
  157.0 1.0 copy-done.3
  158.0 1.5 fusion.1
  159.6 0.7 all-gather.3.cloned.1.call-update
  160.3 64.1 %all-gather.5.cloned.1.call-done = bf16[192,16384]{1,0:T(8,128)(2,1)} async-done(((bf16[192,2048]{1,0:T(8,128)(2,1)}), bf16[192,16384]{1,0:T(8,128)(2,1)}) %all-gather.5.cloned.1.call-update) | async-done | bytes 6291472 | tf_op jit(solution)/shard_map/all_gather | solution.py:23
  224.4 6.3 %copy.12 = bf16[24,4,8,4096]{3,2,0,1:T(8,128)(2,1)} copy(bf16[24,4,8,4096]{3,2,1,0:T(8,128)(2,1)} %bitcast.57) | data formatting | bytes 12582912 | tf_op jit(solution)/shard_map/all_to_all | solution.py:24
  230.7 5.5 %all-to-all-start = ((bf16[192,4,4096]{2,0,1:T(8,128)(2,1)}), bf16[192,4,4096]{2,0,1:T(8,128)(2,1)}, u32[]{:S(2)}, u32[]{:S(2)}) async-start(bf16[192,4,4096]{2,0,1:T(8,128)(2,1)} %bitcast.56), calls=%async_computation | async-start | bytes 12582912 | tf_op jit(solution)/shard_map/all_to_all | solution.py:24
  236.2 90.4 %all-gather.3.cloned.1.call-done = bf16[768,2048]{1,0:T(8,128)(2,1)} async-done(((bf16[192,2048]{1,0:T(8,128)(2,1)}), bf16[768,2048]{1,0:T(8,128)(2,1)}) %all-gather.3.cloned.1.call-update) | async-done | bytes 3145744 | tf_op jit(solution)/shard_map/all_gather | solution.py:22
  326.6 1.8 all-to-all-done
  328.4 22.6 %convolution_multiply_fusion = f32[2048,4096]{1,0:T(8,128)} fusion(bf16[768,2048]{1,0:T(8,128)(2,1)} %all-gather.3.cloned.1.call-done, bf16[768,4096]{1,0:T(8,128)(2,1)} %bitcast.7), kind=kOutput, calls=%fused_computation.2 | convolution fusion | flops 12893290496 | bytes 42991616 | tf_op jit(solution)/shard_map/dot_general | solution.py:25
  (25 shorter events, 0.7 us)
Async XLA Ops:
  7.2 0.9 copy-start
  7.2 81.5 %all-reduce.4.cloned.1.call-start = ((), (), s32[]{:S(2)}) async-start(), calls=%async_computation.3 | async-start | bytes 4718592 | tf_op jit(solution)/shard_map/psum | solution.py:14
  11.9 212.5 %all-gather.5.cloned.1.call-start = ((), (), s32[]{:S(2)}) async-start(), calls=%async_computation.2 | async-start | bytes 7077888 | tf_op jit(solution)/shard_map/all_gather | solution.py:23
  88.7 61.9 %copy-start.4 = (f32[256,2048]{1,0:T(8,128)S(1)}, f32[256,2048]{1,0:T(8,128)}, u32[]{:S(2)}) copy-start(f32[256,2048]{1,0:T(8,128)} %get-tuple-element.18) | copy-start | bytes 6291460
  156.8 1.1 copy-start.3
  158.0 1.6 copy-start.2
  159.6 167.1 %all-gather.3.cloned.1.call-start = ((), (), s32[]{:S(2)}) async-start(), calls=%async_computation.1 | async-start | bytes 3932160 | tf_op jit(solution)/shard_map/all_gather | solution.py:22
  230.7 97.7 %all-to-all-start = ((bf16[192,4,4096]{2,0,1:T(8,128)(2,1)}), bf16[192,4,4096]{2,0,1:T(8,128)(2,1)}, u32[]{:S(2)}, u32[]{:S(2)}) async-start(bf16[192,4,4096]{2,0,1:T(8,128)(2,1)} %bitcast.56), calls=%async_computation | async-start | bytes 12582912 | tf_op jit(solution)/shard_map/all_to_all | solution.py:24
  328.4 22.6 %copy-start.1 = (bf16[192,256]{1,0:T(8,128)(2,1)S(1)}, bf16[192,256]{1,0:T(8,128)(2,1)}, u32[]{:S(2)}) copy-start(bf16[192,256]{1,0:T(8,128)(2,1)} %param.2) | copy-start | bytes 294916
Sparse Core Ops, SparseCore 0:
  12.1 76.5 all-reduce.3
  159.7 64.6 all-gather.4
  226.2 100.3 all-gather.2
where the time goes:
time: 358 us
  waiting for transfers between devices  234 us (65%)
  other arithmetic  54.8 us (15%)
  matrix products  34.6 us (10%)
  between operations  15.2 us (4%)
  local copies, waits for them, and re-layouts  13.4 us (4%)
  starting transfers between devices  5.64 us (2%)
    all_gather x1, waiting for transfers between devices, per_device(): mine = lax.all_gather(residual, 'days', axis=0, tiled=True)  90.4 us
    psum x1, waiting for transfers between devices, per_device(): gram, cross = lax.psum((gram, cross), 'days')  76.7 us
    all_gather x1, waiting for transfers between devices, per_device(): day_block = lax.all_gather(residual, 'assets', axis=1, tiled=True)  64.1 us
    another operation x6, other arithmetic, per_device(): lower = jnp.linalg.cholesky(gram)  34 us
    dot_general x1, matrix products, per_device(): lax.dot_general(mine, columns, (((0,), (0,)), ((), ())), preferred_elemen...  22.6 us
    another operation x4, other arithmetic, per_device(): lax.linalg.triangular_solve(lower, middle, left_side=True, lower=True, tr...  19.8 us
  transfers between devices with their start and end apart: 4, of which 4 were waited for; matrix products, arithmetic and copies ran while one was open for 2% of the time, Pallas kernels for 0%

commit v1 on v0

--- a/solution.py
+++ b/solution.py
@@ -20,7 +20,14 @@
     fitted = jnp.dot(factors, loadings.astype(jnp.bfloat16), preferred_element_type=jnp.float32)
     residual = (returns.astype(jnp.float32) - fitted).astype(jnp.bfloat16)
     mine = lax.all_gather(residual, "days", axis=0, tiled=True)
-    day_block = lax.all_gather(residual, "assets", axis=1, tiled=True)
+    ring = [residual]
+    for hop in range(7):
+        ring.append(lax.ppermute(ring[-1], "assets", [(dev, (dev + 1) % 8) for dev in range(8)]))
+    day_block = jnp.roll(
+        jnp.concatenate(ring[::-1], axis=1),
+        (lax.axis_index("assets") + 1) * ring[0].shape[1],
+        axis=1,
+    )
     columns = lax.all_to_all(day_block, "days", split_axis=1, concat_axis=0, tiled=True)
     covariance = lax.dot_general(
         mine, columns, (((0,), (0,)), ((), ())), preferred_element_type=jnp.float32

time: 358 us -> 387 us (1.081)
  local copies, waits for them, and re-layouts: 13.4 us -> 43.4 us
  waiting for transfers between devices: 234 us -> 229 us
    ppermute x0 -> x7, waiting for transfers between devices: none -> 92.8 us  [per_device(): lax.ppermute(ring[-1], 'assets', [(dev, (dev + 1) % 8) for dev in range(8)])]
    all_gather x1, waiting for transfers between devices: 90.4 us -> 0.02 us  [per_device(): mine = lax.all_gather(residual, 'days', axis=0, tiled=True)]
    all_gather x1 -> x0, waiting for transfers between devices: 64.1 us -> none  [per_device(): day_block = lax.all_gather(residual, 'assets', axis=1, tiled=True)]
    all_to_all x1, waiting for transfers between devices: 1.8 us -> 59.5 us  [per_device(): lax.all_to_all(day_block, 'days', split_axis=1, concat_axis=0, tiled=True)]
    unnamed x10 -> x45, local copies, waits for them, and re-layouts: 1.84 us -> 31 us
  transfers between devices with their start and end apart: 4 -> 10, of which waited for: 4 -> 9; matrix products, arithmetic and copies ran while one was open for 2% -> 9% of each run, Pallas kernels for 0% -> 0%
where the time goes in v1:
time: 387 us; the launch traced here: 386 us
  waiting for transfers between devices  229 us (59%)
  other arithmetic  54.8 us (14%)
  local copies, waits for them, and re-layouts  43.4 us (11%)
  matrix products  37.6 us (10%)
  between operations  15.6 us (4%)
  starting transfers between devices  5.62 us (1%)
    ppermute x7, waiting for transfers between devices, per_device(): lax.ppermute(ring[-1], 'assets', [(dev, (dev + 1) % 8) for dev in range(8)])  92.8 us
    psum x1, waiting for transfers between devices, per_device(): gram, cross = lax.psum((gram, cross), 'days')  76.7 us
    all_to_all x1, waiting for transfers between devices, per_device(): lax.all_to_all(day_block, 'days', split_axis=1, concat_axis=0, tiled=True)  59.5 us
    another operation x6, other arithmetic, per_device(): lower = jnp.linalg.cholesky(gram)  34 us
    unnamed x45, local copies, waits for them, and re-layouts  31 us
    dot_general x1, matrix products, per_device(): lax.dot_general(mine, columns, (((0,), (0,)), ((), ())), preferred_elemen...  22.6 us
    another operation x4, other arithmetic, per_device(): lax.linalg.triangular_solve(lower, middle, left_side=True, lower=True, tr...  19.8 us
  transfers between devices with their start and end apart: 10, of which 9 were waited for; matrix products, arithmetic and copies ran while one was open for 9% of the time, Pallas kernels for 0%

profile of v1, /device:TPU:0, one launch (start us, length us, event | category | flops | bytes accessed | tf_op | source)
XLA Modules:
  0.0 386.3 jit_solution(2429920080524293062)
XLA Ops:
  9.0 2.9 fusion.16
  12.0 76.7 %all-reduce.4.cloned.1.call-done = (f32[256,2048]{1,0:T(8,128)}, f32[256,256]{0,1:T(8,128)}) async-done(((f32[256,2048]{1,0:T(8,128)}, f32[256,256]{0,1:T(8,128)}), (f32[256,2048]{1,0:T(8,128)}, f32[256,256]{0,1:T(8,128)})) %all-reduce.4.cloned.1.call-update) | async-done | bytes 2359312 | tf_op jit(solution)/shard_map/psum | solution.py:14
  90.8 11.7 %cholesky.50 = f32[128,128]{1,0:T(8,128)S(1)} custom-call(f32[128,128]{1,0:T(8,128)S(1)} %cholesky.118), custom_call_target="Cholesky" | custom-call | tf_op jit(solution)/shard_map/jit(cholesky)/cholesky | solution.py:15
  102.5 9.8 %custom-call.16 = f32[1,128,128]{1,2,0:T(8,128)S(1)} custom-call(f32[1,128,128]{2,1,0:T(8,128)S(1)} %get-tuple-element.25), custom_call_target="InvertDiagBlocksLowerTriangular" | custom-call | tf_op jit(solution)/shard_map/jit(cholesky)/cholesky | solution.py:15
  112.8 11.7 %cholesky.105 = f32[128,128]{1,0:T(8,128)S(1)} custom-call(f32[128,128]{1,0:T(8,128)S(1)} %convolution_subtract_fusion.2), custom_call_target="Cholesky" | custom-call | tf_op jit(solution)/shard_map/jit(cholesky)/cholesky | solution.py:15
  126.6 4.1 %while.1 = (s32[]{:T(128)}, f32[256,256]{1,0:T(8,128)S(1)}, s32[2,2]{1,0:T(2,128)S(1)}, f32[2,128,128]{2,1,0:T(8,128)S(1)}, s32[]{:T(128)}) while((s32[]{:T(128)}, f32[256,256]{1,0:T(8,128)S(1)}, s32[2,2]{1,0:T(2,128)S(1)}, f32[2,128,128]{2,1,0:T(8,128)S(1)}, s32[]{:T(128)}) %tuple.27), condition=%wide.while_cond, body=%wide.while_body.sunk | while | flops 2 | bytes 131189 | solution.py:17
  130.8 19.7 %custom-call.17 = f32[2,128,128]{1,2,0:T(8,128)S(1)} custom-call(f32[2,128,128]{2,1,0:T(8,128)S(1)} %get-tuple-element.9), custom_call_target="InvertDiagBlocksLowerTriangular" | custom-call | tf_op jit(solution)/shard_map/triangular_solve | solution.py:17
  150.5 2.3 fusion.2
  152.7 2.2 convolution_subtract_fusion.1
  159.3 2.1 fusion.1
  161.5 13.2 %collective-permute-done = bf16[192,2048]{1,0:T(8,128)(2,1)S(1)} collective-permute-done((bf16[192,2048]{1,0:T(8,128)(2,1)S(1)}, bf16[192,2048]{1,0:T(8,128)(2,1)S(1)}, u32[]{:S(2)}, u32[]{:S(2)}) %collective-permute-start) | collective-permute-done | bytes 786464 | tf_op jit(solution)/shard_map/ppermute | solution.py:25
  175.5 13.2 %collective-permute-done.1 = bf16[192,2048]{1,0:T(8,128)(2,1)S(1)} collective-permute-done((bf16[192,2048]{1,0:T(8,128)(2,1)S(1)}, bf16[192,2048]{1,0:T(8,128)(2,1)S(1)}, u32[]{:S(2)}, u32[]{:S(2)}) %collective-permute-start.1) | collective-permute-done | bytes 786464 | tf_op jit(solution)/shard_map/ppermute | solution.py:25
  189.7 13.2 %collective-permute-done.2 = bf16[192,2048]{1,0:T(8,128)(2,1)S(1)} collective-permute-done((bf16[192,2048]{1,0:T(8,128)(2,1)S(1)}, bf16[192,2048]{1,0:T(8,128)(2,1)S(1)}, u32[]{:S(2)}, u32[]{:S(2)}) %collective-permute-start.2) | collective-permute-done | bytes 786464 | tf_op jit(solution)/shard_map/ppermute | solution.py:25
  203.8 13.2 %collective-permute-done.3 = bf16[192,2048]{1,0:T(8,128)(2,1)S(1)} collective-permute-done((bf16[192,2048]{1,0:T(8,128)(2,1)S(1)}, bf16[192,2048]{1,0:T(8,128)(2,1)S(1)}, u32[]{:S(2)}, u32[]{:S(2)}) %collective-permute-start.3) | collective-permute-done | bytes 786464 | tf_op jit(solution)/shard_map/ppermute | solution.py:25
  217.9 13.2 %collective-permute-done.4 = bf16[192,2048]{1,0:T(8,128)(2,1)S(1)} collective-permute-done((bf16[192,2048]{1,0:T(8,128)(2,1)S(1)}, bf16[192,2048]{1,0:T(8,128)(2,1)S(1)}, u32[]{:S(2)}, u32[]{:S(2)}) %collective-permute-start.4) | collective-permute-done | bytes 786464 | tf_op jit(solution)/shard_map/ppermute | solution.py:25
  232.0 13.3 %collective-permute-done.5 = bf16[192,2048]{1,0:T(8,128)(2,1)} collective-permute-done((bf16[192,2048]{1,0:T(8,128)(2,1)S(1)}, bf16[192,2048]{1,0:T(8,128)(2,1)}, u32[]{:S(2)}, u32[]{:S(2)}) %collective-permute-start.5) | collective-permute-done | bytes 786464 | tf_op jit(solution)/shard_map/ppermute | solution.py:25
  245.4 13.4 %collective-permute-done.6 = bf16[192,2048]{1,0:T(8,128)(2,1)} collective-permute-done((bf16[192,2048]{1,0:T(8,128)(2,1)}, bf16[192,2048]{1,0:T(8,128)(2,1)}, u32[]{:S(2)}, u32[]{:S(2)}) %collective-permute-start.6) | collective-permute-done | bytes 786464 | tf_op jit(solution)/shard_map/ppermute | solution.py:25
  258.8 2.1 constant_dynamic-update-slice_fusion.15
  260.9 2.1 constant_dynamic-update-slice_fusion.14
  263.0 2.1 constant_dynamic-update-slice_fusion.13
  265.1 2.1 constant_dynamic-update-slice_fusion.12
  267.2 2.1 constant_dynamic-update-slice_fusion.11
  269.3 2.1 constant_dynamic-update-slice_fusion.10
  271.4 2.1 constant_dynamic-update-slice_fusion.9
  273.4 2.1 constant_dynamic-update-slice_fusion.8
  275.5 2.1 constant_dynamic-update-slice_fusion.7
  277.6 2.1 constant_dynamic-update-slice_fusion.6
  285.5 3.2 constant_dynamic-slice_fusion.1
  288.7 3.1 copy.17
  291.8 5.5 %all-to-all-start = ((bf16[192,4,4096]{2,0,1:T(8,128)(2,1)}), bf16[192,4,4096]{2,0,1:T(8,128)(2,1)}, u32[]{:S(2)}, u32[]{:S(2)}) async-start(bf16[192,4,4096]{2,0,1:T(8,128)(2,1)} %bitcast.56), calls=%async_computation | async-start | bytes 12582912 | tf_op jit(solution)/shard_map/all_to_all | solution.py:31
  297.3 59.5 %all-to-all-done = bf16[192,4,4096]{2,0,1:T(8,128)(2,1)} async-done(((bf16[192,4,4096]{2,0,1:T(8,128)(2,1)}), bf16[192,4,4096]{2,0,1:T(8,128)(2,1)}, u32[]{:S(2)}, u32[]{:S(2)}) %all-to-all-start) | async-done | bytes 6291488 | tf_op jit(solution)/shard_map/all_to_all | solution.py:31
  356.8 22.6 %convolution_multiply_fusion = f32[2048,4096]{1,0:T(8,128)} fusion(bf16[768,2048]{1,0:T(8,128)(2,1)} %all-gather.2.cloned.1.call-done, bf16[768,4096]{1,0:T(8,128)(2,1)} %bitcast.7), kind=kOutput, calls=%fused_computation.2 | convolution fusion | flops 12893290496 | bytes 42991616 | tf_op jit(solution)/shard_map/dot_general | solution.py:32
  (73 shorter events, 23.8 us)
Async XLA Ops:
  7.2 0.9 copy-start
  7.2 81.5 %all-reduce.4.cloned.1.call-start = ((), (), s32[]{:S(2)}) async-start(), calls=%async_computation.2 | async-start | bytes 4718592 | tf_op jit(solution)/shard_map/psum | solution.py:14
  11.9 285.4 %all-gather.2.cloned.1.call-start = ((), (), s32[]{:S(2)}) async-start(), calls=%async_computation.1 | async-start | bytes 3932160 | tf_op jit(solution)/shard_map/all_gather | solution.py:22
  159.3 124.3 %copy-start.4 = (f32[256,2048]{1,0:T(8,128)}, f32[256,2048]{1,0:T(8,128)S(1)}, u32[]{:S(2)}) copy-start(f32[256,2048]{1,0:T(8,128)S(1)} %pad_maximum_fusion) | copy-start | bytes 6291460
  161.4 83.9 %copy-start.2 = (bf16[192,2048]{1,0:T(8,128)(2,1)}, bf16[192,2048]{1,0:T(8,128)(2,1)S(1)}, u32[]{:S(2)}) copy-start(bf16[192,2048]{1,0:T(8,128)(2,1)S(1)} %fusion.1) | copy-start | bytes 2359300
  161.4 13.3 %collective-permute-start = (bf16[192,2048]{1,0:T(8,128)(2,1)S(1)}, bf16[192,2048]{1,0:T(8,128)(2,1)S(1)}, u32[]{:S(2)}, u32[]{:S(2)}) collective-permute-start(bf16[192,2048]{1,0:T(8,128)(2,1)S(1)} %fusion.1), channel_id=1, source_target_pairs={{0,1},{1,2},{2,3},{3,4},{4,5},{5,6},{6,7},{7,0},{8,9},{9,10},{10,1... | collective-permute-start | bytes 2359304 | tf_op jit(solution)/shard_map/ppermute | solution.py:25
  174.7 0.9 copy-start.5
  175.5 13.2 %collective-permute-start.1 = (bf16[192,2048]{1,0:T(8,128)(2,1)S(1)}, bf16[192,2048]{1,0:T(8,128)(2,1)S(1)}, u32[]{:S(2)}, u32[]{:S(2)}) collective-permute-start(bf16[192,2048]{1,0:T(8,128)(2,1)S(1)} %collective-permute-done), channel_id=1, source_target_pairs={{0,1},{1,2},{2,3},{3,4},{4,5},{5,6},{6,7},{7,0},{8,9},{9,10},{10,1... | collective-permute-start | bytes 2359304 | tf_op jit(solution)/shard_map/ppermute | solution.py:25
  188.8 0.9 copy-start.7
  189.7 13.2 %collective-permute-start.2 = (bf16[192,2048]{1,0:T(8,128)(2,1)S(1)}, bf16[192,2048]{1,0:T(8,128)(2,1)S(1)}, u32[]{:S(2)}, u32[]{:S(2)}) collective-permute-start(bf16[192,2048]{1,0:T(8,128)(2,1)S(1)} %collective-permute-done.1), channel_id=1, source_target_pairs={{0,1},{1,2},{2,3},{3,4},{4,5},{5,6},{6,7},{7,0},{8,9},{9,10},{10,1... | collective-permute-start | bytes 2359304 | tf_op jit(solution)/shard_map/ppermute | solution.py:25
  202.9 0.9 copy-start.9
  203.8 13.2 %collective-permute-start.3 = (bf16[192,2048]{1,0:T(8,128)(2,1)S(1)}, bf16[192,2048]{1,0:T(8,128)(2,1)S(1)}, u32[]{:S(2)}, u32[]{:S(2)}) collective-permute-start(bf16[192,2048]{1,0:T(8,128)(2,1)S(1)} %collective-permute-done.2), channel_id=1, source_target_pairs={{0,1},{1,2},{2,3},{3,4},{4,5},{5,6},{6,7},{7,0},{8,9},{9,10},{10,1... | collective-permute-start | bytes 2359304 | tf_op jit(solution)/shard_map/ppermute | solution.py:25
  217.0 0.9 copy-start.11
  217.9 13.2 %collective-permute-start.4 = (bf16[192,2048]{1,0:T(8,128)(2,1)S(1)}, bf16[192,2048]{1,0:T(8,128)(2,1)S(1)}, u32[]{:S(2)}, u32[]{:S(2)}) collective-permute-start(bf16[192,2048]{1,0:T(8,128)(2,1)S(1)} %collective-permute-done.3), channel_id=1, source_target_pairs={{0,1},{1,2},{2,3},{3,4},{4,5},{5,6},{6,7},{7,0},{8,9},{9,10},{10,1... | collective-permute-start | bytes 2359304 | tf_op jit(solution)/shard_map/ppermute | solution.py:25
  231.1 0.9 copy-start.13
  232.0 13.3 %collective-permute-start.5 = (bf16[192,2048]{1,0:T(8,128)(2,1)S(1)}, bf16[192,2048]{1,0:T(8,128)(2,1)}, u32[]{:S(2)}, u32[]{:S(2)}) collective-permute-start(bf16[192,2048]{1,0:T(8,128)(2,1)S(1)} %collective-permute-done.4), channel_id=1, source_target_pairs={{0,1},{1,2},{2,3},{3,4},{4,5},{5,6},{6,7},{7,0},{8,9},{9,10},{10,1... | collective-permute-start | bytes 2359304 | tf_op jit(solution)/shard_map/ppermute | solution.py:25
  245.3 13.5 %collective-permute-start.6 = (bf16[192,2048]{1,0:T(8,128)(2,1)}, bf16[192,2048]{1,0:T(8,128)(2,1)}, u32[]{:S(2)}, u32[]{:S(2)}) collective-permute-start(bf16[192,2048]{1,0:T(8,128)(2,1)} %collective-permute-done.5), channel_id=1, source_target_pairs={{0,1},{1,2},{2,3},{3,4},{4,5},{5,6},{6,7},{7,0},{8,9},{9,10},{10,1... | collective-permute-start | bytes 2359304 | tf_op jit(solution)/shard_map/ppermute | solution.py:25
  245.3 34.4 %copy-start.14 = (bf16[192,2048]{1,0:T(8,128)(2,1)S(1)}, bf16[192,2048]{1,0:T(8,128)(2,1)}, u32[]{:S(2)}) copy-start(bf16[192,2048]{1,0:T(8,128)(2,1)} %copy-done.13) | copy-start | bytes 2359300
  245.3 35.3 %copy-start.12 = (bf16[192,2048]{1,0:T(8,128)(2,1)S(1)}, bf16[192,2048]{1,0:T(8,128)(2,1)}, u32[]{:S(2)}) copy-start(bf16[192,2048]{1,0:T(8,128)(2,1)} %copy-done.11) | copy-start | bytes 2359300
  245.3 36.3 %copy-start.10 = (bf16[192,2048]{1,0:T(8,128)(2,1)S(1)}, bf16[192,2048]{1,0:T(8,128)(2,1)}, u32[]{:S(2)}) copy-start(bf16[192,2048]{1,0:T(8,128)(2,1)} %copy-done.9) | copy-start | bytes 2359300
  245.4 37.2 %copy-start.8 = (bf16[192,2048]{1,0:T(8,128)(2,1)S(1)}, bf16[192,2048]{1,0:T(8,128)(2,1)}, u32[]{:S(2)}) copy-start(bf16[192,2048]{1,0:T(8,128)(2,1)} %copy-done.7) | copy-start | bytes 2359300
  245.4 38.2 %copy-start.6 = (bf16[192,2048]{1,0:T(8,128)(2,1)S(1)}, bf16[192,2048]{1,0:T(8,128)(2,1)}, u32[]{:S(2)}) copy-start(bf16[192,2048]{1,0:T(8,128)(2,1)} %copy-done.5) | copy-start | bytes 2359300
  245.4 39.1 %copy-start.3 = (bf16[192,2048]{1,0:T(8,128)(2,1)S(1)}, bf16[192,2048]{1,0:T(8,128)(2,1)}, u32[]{:S(2)}) copy-start(bf16[192,2048]{1,0:T(8,128)(2,1)} %copy-done.2) | copy-start | bytes 2359300
  291.8 65.0 %all-to-all-start = ((bf16[192,4,4096]{2,0,1:T(8,128)(2,1)}), bf16[192,4,4096]{2,0,1:T(8,128)(2,1)}, u32[]{:S(2)}, u32[]{:S(2)}) async-start(bf16[192,4,4096]{2,0,1:T(8,128)(2,1)} %bitcast.56), calls=%async_computation | async-start | bytes 12582912 | tf_op jit(solution)/shard_map/all_to_all | solution.py:31
  356.8 22.6 %copy-start.1 = (bf16[192,256]{1,0:T(8,128)(2,1)S(1)}, bf16[192,256]{1,0:T(8,128)(2,1)}, u32[]{:S(2)}) copy-start(bf16[192,256]{1,0:T(8,128)(2,1)} %param.2) | copy-start | bytes 294916
Sparse Core Ops, SparseCore 0:
  12.1 76.5 all-reduce.3
  245.4 44.1 all-gather.1
